TPU v7x, 32 devices: a whole 2x2x4 slice. The times are simulated.
32 devices in a mesh: dp: 8 (over y, x, core), seq: 4 (over z).
Axes of the slice: x: 2, y: 2, z: 4, core: 2. Of those that a mesh axis runs over, the one named last changes fastest.
Arguments:
- queries: bfloat16 [8192, 8192], P(('dp', 'seq')), may hold values from -60 to 60
- keys: bfloat16 [8192, 1024], P(('dp', 'seq')), may hold values from -60 to 60
- values: bfloat16 [8192, 1024], P(('dp', 'seq')), may hold values from -6 to 6
- plan: int32 [8192], P(('dp', 'seq')), may hold values from 0 to 8191, as said below
- segment_ids: int32 [8192], P(('dp', 'seq')), may hold values from 0 to 63, as said below
Outputs:
- attended: bfloat16 [8192, 8192], P(('dp', 'seq'))
Inputs may be any that keep to these rules, and one draw needn't show every extreme that they name: `plan`: A permutation of the owner rows. The rows of one device go exactly 8 to each device (owner rows d * 256 to (d + 1) * 256 - 1 belong to device d), in random order among the device's rows. `segment_ids`: documents are runs of equal ids that never fall; every length is a multiple of 128; no document crosses a boundary of the aligned blocks of 1024 owner rows; one document fills a whole block.
All inputs are finite; a program needn't handle non-finite values.
Results may differ from a plain program's by a relative error of at most 0.0053.
Values may be sent and summed in bfloat16 or wider, within the bound.
A program may use at most 128 MiB of HBM per device.

v0:
```python
import functools

import jax
import jax.numpy as jnp
import numpy as np
from jax import lax
from jax.experimental import pallas as pl
from jax.experimental.pallas import tpu as pltpu
from jax.sharding import PartitionSpec as P

H = 64
KVH = 8
HD = 128
theta_base = 500000.0
UNIT = 128
META = 128
LOG2E = 1.4426950408889634


def dot(a, b):
    return jnp.dot(a, b, preferred_element_type=jnp.float32)


def turn(x, c, s):
    return (x * c + pltpu.roll(x, HD // 2, 1) * s).astype(jnp.bfloat16)


def restore(onehot, home, out):
    out[...] = lax.dot_general(
        onehot[...], home[...], (((0,), (0,)), ((), ())), preferred_element_type=jnp.float32
    ).astype(jnp.bfloat16)


def travel(
    seqs, dps, q, k, v, plan, seg, freqs, home, onehot,
    qs, kvs, metas, qr, kvz, metaz, ob, ks, vs, kmeta, cq, sq, ck, sk, bias, part_q,
    kv_send, kv_recv, kv_own, q_send, q_recv, q_own, q_load, o_send, o_recv, o_own,
    m_send, m_recv, m_own, mz_send, mz_recv, z_send, z_recv,
):
    rows = q.shape[0]
    per_kv = H // KVH
    wide = per_kv * HD
    chunk = rows // seqs
    share = chunk // dps
    slab = rows // dps
    group = rows * seqs
    upd = rows // UNIT
    me = lax.axis_index("dp")
    z = lax.axis_index("seq")

    def remote(src, dst, send, recv, where):
        return pltpu.make_async_remote_copy(
            src_ref=src, dst_ref=dst, send_sem=send, recv_sem=recv,
            device_id=where, device_id_type=pl.DeviceIdType.MESH,
        )

    def slab_of(d):
        return pl.ds(pl.multiple_of(d * slab, slab), slab)

    def cols(h, width):
        return pl.ds(pl.multiple_of(h * width, width), width)

    barrier = pltpu.get_barrier_semaphore()
    peers = [lax.rem(me + k, dps) for k in range(1, dps)]
    planes = [lax.rem(z + k, seqs) for k in range(1, seqs)]
    for d in peers:
        pl.semaphore_signal(
            barrier, inc=1, device_id=(d, z), device_id_type=pl.DeviceIdType.MESH
        )
    for p in planes:
        pl.semaphore_signal(
            barrier, inc=1, device_id=(me, p), device_id_type=pl.DeviceIdType.MESH
        )

    def q_in(h):
        return pltpu.make_async_copy(q.at[:, cols(h, wide)], qs.at[h], q_load.at[h])

    @pl.loop(0, KVH)
    def _(h):
        q_in(h).start()

    row = lax.broadcasted_iota(jnp.int32, (rows, rows), 0)
    col = lax.broadcasted_iota(jnp.int32, (rows, rows), 1)
    eye = jnp.where(row == col, 1.0, 0.0).astype(jnp.bfloat16)
    target = (plan[...] // rows).astype(jnp.float32)
    spread = jnp.broadcast_to(target, (16, rows)).astype(jnp.bfloat16)
    across = (((1,), (1,)), ((), ()))
    upright = lax.dot_general(eye, spread, across, preferred_element_type=jnp.float32)[:, 0:1]
    ahead = jnp.where((upright == target) & (row < col), 1.0, 0.0)
    slot = target * share + jnp.sum(ahead, axis=0, keepdims=True)
    onehot[...] = jnp.where(slot == row.astype(jnp.float32), 1.0, 0.0).astype(jnp.bfloat16)
    spot_row = plan[...] % group
    lines = lax.broadcasted_iota(jnp.int32, (META, rows), 0)
    high = (spot_row // 32).astype(jnp.float32)
    low = (spot_row % 32).astype(jnp.float32)
    lines = jnp.where(lines == 0, high, jnp.where(lines == 1, low, 0.0)).astype(jnp.bfloat16)
    metas[...] = lax.dot_general(
        onehot[...], lines, across, preferred_element_type=jnp.float32
    ).astype(jnp.bfloat16)
    lane = lax.broadcasted_iota(jnp.int32, (1, META), 1)
    marks = jnp.zeros((1, META), jnp.float32)
    for u in range(upd):
        marks = jnp.where(lane == u, seg[0:1, u * UNIT : u * UNIT + 1].astype(jnp.float32), marks)
    metaz[z, rows : rows + 16, :] = jnp.broadcast_to(marks, (16, META)).astype(jnp.bfloat16)

    pl.semaphore_wait(barrier, dps + seqs - 2)

    most = pl.ds(0, rows - slab)
    for d in peers:
        remote(
            metas.at[slab_of(d)], metaz.at[z, slab_of(me)], m_send, m_recv, (d, z)
        ).start()
    m_copy = pltpu.make_async_copy(metas.at[slab_of(me)], metaz.at[z, slab_of(me)], m_own)
    m_copy.start()

    def kv_local(h):
        return pltpu.make_async_copy(
            kvs.at[h, slab_of(me)], kvz.at[z, h, slab_of(me)], kv_own.at[h]
        )

    def q_local(h):
        return pltpu.make_async_copy(
            qs.at[h, slab_of(me)], qr.at[h, slab_of(me)], q_own.at[h]
        )

    def o_local(h):
        return pltpu.make_async_copy(
            ob.at[h, slab_of(me)], home.at[slab_of(me), cols(h, wide)], o_own.at[h]
        )

    @pl.loop(0, KVH)
    def _(h):
        both = jnp.concatenate([k[:, cols(h, HD)], v[:, cols(h, HD)]], axis=1)
        kvs[h] = dot(onehot[...], both).astype(jnp.bfloat16)
        for d in peers:
            remote(
                kvs.at[h, slab_of(d)], kvz.at[z, h, slab_of(me)],
                kv_send.at[h], kv_recv.at[h], (d, z),
            ).start()
        kv_local(h).start()

    def q_out(h):
        q_in(h).wait()
        qs[h] = dot(onehot[...], qs[h]).astype(jnp.bfloat16)
        for d in peers:
            remote(
                qs.at[h, slab_of(d)], qr.at[h, slab_of(me)],
                q_send.at[h], q_recv.at[h], (d, z),
            ).start()
        q_local(h).start()

    def meta_all():
        return remote(metaz.at[z, most], metaz.at[z, most], m_send, m_recv, (me, z))

    def kv_all(h):
        return remote(
            kvz.at[z, h, most], kvz.at[z, h, most], kv_send.at[h], kv_recv.at[h], (me, z)
        )

    def q_all(h):
        return remote(qr.at[h, most], qr.at[h, most], q_send.at[h], q_recv.at[h], (me, z))

    def o_all(h):
        place = home.at[most, cols(h, wide)]
        return remote(ob.at[h, most], place, o_send.at[h], o_recv.at[h], (me, z))

    meta_all().wait_recv()
    m_copy.wait()

    def meta_hop(k, p, origin):
        return remote(
            metaz.at[origin], metaz.at[origin], mz_send.at[k - 1], mz_recv.at[origin], (me, p)
        )

    for k, p in enumerate(planes, 1):
        meta_hop(k, p, z).start()

    def arrival(s):
        inner = s % chunk
        return (inner // share) * (seqs * share) + (s // chunk) * share + inner % share

    sort = jnp.where(col == arrival(row), 1.0, 0.0).astype(jnp.bfloat16)
    unsort = jnp.where(row == arrival(col), 1.0, 0.0).astype(jnp.bfloat16)

    def prepare():
        for k, p in enumerate(planes, 1):
            meta_hop(k, p, p).wait_recv()
        ids = []
        for p in range(seqs):
            line = metaz[p, rows : rows + 16, :].astype(jnp.float32)
            ids += [line[0:1, u : u + 1] for u in range(upd)]
        sign = jnp.where(lane < HD // 2, -1.0, 1.0)

        def spots(sorted_meta):
            spot = sorted_meta[:, 0:1] * 32.0 + sorted_meta[:, 1:2]
            mine = jnp.zeros_like(spot)
            for u in range(len(ids)):
                inside = (spot >= u * UNIT) & (spot < (u + 1) * UNIT)
                mine = jnp.where(inside, ids[u], mine)
            first = jnp.full_like(spot, float(group))
            for u in range(len(ids)):
                first = jnp.where(mine == ids[u], jnp.minimum(first, float(u * UNIT)), first)
            angles = (spot - first) * freqs[0:1, :]
            return spot, first, jnp.cos(angles), jnp.sin(angles) * sign

        for p in range(seqs):
            sorted_meta = dot(sort, metaz[p, :rows, :])
            _, _, ck[p], sk[p] = spots(sorted_meta)
            narrow = sorted_meta.astype(jnp.bfloat16)
            for c in range(seqs):
                kmeta[c * rows + p * chunk : c * rows + (p + 1) * chunk] = narrow[
                    c * chunk : (c + 1) * chunk
                ]
        spot, first, cq[...], sq[...] = spots(dot(sort, metaz[z, :rows, :]))
        weigh = jnp.where(lane == 0, 32.0, jnp.where(lane == 1, 1.0, 0.0))
        weigh = jnp.broadcast_to(weigh, (16, META)).astype(jnp.bfloat16)
        key = lax.dot_general(
            weigh, kmeta[...], (((1,), (1,)), ((), ())), preferred_element_type=jnp.float32
        )[0:1, :]
        bias[...] = jnp.where((key <= spot) & (key >= first), 0.0, -1e30)

    def attend(h):
        for p in range(seqs):
            both = dot(sort, kvz[p, h])
            part = turn(both[:, :HD], ck[p], sk[p])
            part_v = both[:, HD:].astype(jnp.bfloat16)
            for c in range(seqs):
                place = slice(c * rows + p * chunk, c * rows + (p + 1) * chunk)
                ks[place] = part[c * chunk : (c + 1) * chunk]
                vs[place] = part_v[c * chunk : (c + 1) * chunk]
        x = dot(sort, qr[h])
        turned = [turn(x[:, g * HD : (g + 1) * HD], cq[...], sq[...]) for g in range(per_kv)]
        for c in range(seqs):
            reach = (c + 1) * rows
            block = jnp.concatenate([t[c * chunk : (c + 1) * chunk] for t in turned], axis=0)
            s = lax.dot_general(
                block, ks[:reach], (((1,), (1,)), ((), ())), preferred_element_type=jnp.float32
            )
            s = s.reshape(per_kv, chunk, reach) * (HD ** -0.5 * LOG2E)
            s = s + bias[c * chunk : (c + 1) * chunk, :reach][None]
            e = jnp.exp2(s - jnp.max(s, axis=-1, keepdims=True))
            total = jnp.sum(e, axis=-1, keepdims=True).reshape(per_kv * chunk, 1)
            mixed = dot(e.astype(jnp.bfloat16).reshape(per_kv * chunk, reach), vs[:reach])
            mixed = (mixed / total).astype(jnp.bfloat16)
            for g in range(per_kv):
                part_q[c * chunk : (c + 1) * chunk, g * HD : (g + 1) * HD] = mixed[
                    g * chunk : (g + 1) * chunk
                ]
        ob[h] = dot(unsort, part_q[...]).astype(jnp.bfloat16)

    def hop(up, t, origin, h):
        step = 1 if up else -1
        return remote(
            kvz.at[origin, h], kvz.at[origin, h],
            z_send.at[(0 if up else 1) * seqs + t, h], z_recv.at[origin, h], (me, z + step),
        )

    @pl.loop(0, KVH + seqs - 1)
    def _(i):
        @pl.when(i < KVH)
        def _():
            kv_all(i).wait_recv()
            kv_local(i).wait()

            @pl.when(z + 1 < seqs)
            def _():
                hop(True, 0, z, i).start()

            @pl.when(z > 0)
            def _():
                hop(False, 0, z, i).start()

        for t in range(1, seqs):
            live = (i >= t) & (i - t < KVH)

            @pl.when(live & (z >= t))
            def _():
                hop(True, t, z - t, i - t).wait_recv()

                @pl.when(z + 1 < seqs)
                def _():
                    hop(True, t, z - t, i - t).start()

            @pl.when(live & (z + t < seqs))
            def _():
                hop(False, t, z + t, i - t).wait_recv()

                @pl.when(z > 0)
                def _():
                    hop(False, t, z + t, i - t).start()

        @pl.when(i < KVH // 2)
        def _():
            q_out(2 * i)
            q_out(2 * i + 1)

        @pl.when(i == min(2, seqs - 1))
        def _():
            prepare()

        @pl.when(i >= seqs - 1)
        def _():
            h = i - (seqs - 1)
            q_all(h).wait_recv()
            q_local(h).wait()
            attend(h)
            for d in peers:
                remote(
                    ob.at[h, slab_of(d)], home.at[slab_of(me), cols(h, wide)],
                    o_send.at[h], o_recv.at[h], (d, z),
                ).start()
            o_local(h).start()

    meta_all().wait_send()
    for k, p in enumerate(planes, 1):
        meta_hop(k, p, z).wait_send()

    @pl.loop(0, KVH)
    def _(h):
        kv_all(h).wait_send()
        q_all(h).wait_send()
        for t in range(seqs - 1):

            @pl.when((z >= t) & (z + 1 < seqs))
            def _():
                hop(True, t, z - t, h).wait_send()

            @pl.when((z + t < seqs) & (z > 0))
            def _():
                hop(False, t, z + t, h).wait_send()

        o_all(h).wait_send()
        o_all(h).wait_recv()
        o_local(h).wait()


def per_device(queries, keys, values, plan, segment_ids):
    rows = queries.shape[0]
    seqs = lax.axis_size("seq")
    dps = lax.axis_size("dp")
    group = rows * seqs
    share = rows // (seqs * dps)
    chunk = rows // seqs
    per_kv = H // KVH
    exponents = np.arange(HD // 2, dtype=np.float32)
    freqs = np.float32(theta_base) ** (np.float32(-2.0) * exponents / np.float32(HD))
    freqs = jnp.asarray(np.broadcast_to(np.concatenate([freqs, freqs])[None, :], (8, HD)))
    anywhere = pl.BlockSpec(memory_space=pl.ANY)
    inside = pl.BlockSpec(memory_space=pltpu.VMEM)
    dma = pltpu.SemaphoreType.DMA
    bf16, f32 = jnp.bfloat16, jnp.float32
    home, onehot = pl.pallas_call(
        functools.partial(travel, seqs, dps),
        in_specs=[anywhere, inside, inside, inside, inside, inside],
        out_specs=(anywhere, inside),
        out_shape=(
            jax.ShapeDtypeStruct(queries.shape, bf16),
            jax.ShapeDtypeStruct((rows, rows), bf16),
        ),
        scratch_shapes=[
            pltpu.VMEM((KVH, rows, per_kv * HD), bf16),
            pltpu.VMEM((KVH, rows, 2 * HD), bf16),
            pltpu.VMEM((rows, META), bf16),
            pltpu.VMEM((KVH, rows, per_kv * HD), bf16),
            pltpu.VMEM((seqs, KVH, rows, 2 * HD), bf16),
            pltpu.VMEM((seqs, rows + 16, META), bf16),
            pltpu.VMEM((KVH, rows, per_kv * HD), bf16),
            pltpu.VMEM((group, HD), bf16),
            pltpu.VMEM((group, HD), bf16),
            pltpu.VMEM((group, META), bf16),
            pltpu.VMEM((rows, HD), f32),
            pltpu.VMEM((rows, HD), f32),
            pltpu.VMEM((seqs, rows, HD), f32),
            pltpu.VMEM((seqs, rows, HD), f32),
            pltpu.VMEM((rows, group), f32),
            pltpu.VMEM((rows, per_kv * HD), bf16),
            dma((KVH,)), dma((KVH,)), dma((KVH,)),
            dma((KVH,)), dma((KVH,)), dma((KVH,)),
            dma((KVH,)), dma((KVH,)), dma((KVH,)), dma((KVH,)),
            dma, dma, dma, dma((seqs,)), dma((seqs,)),
            dma((2 * seqs, KVH)), dma((seqs, KVH)),
        ],
        compiler_params=pltpu.CompilerParams(
            collective_id=0, has_side_effects=True, vmem_limit_bytes=56 * 1024 * 1024
        ),
    )(queries, keys, values, plan[None, :], segment_ids[None, :], freqs)
    block = pl.BlockSpec((rows, per_kv * HD), lambda h: (0, h))
    return pl.pallas_call(
        restore,
        grid=(KVH,),
        in_specs=[pl.BlockSpec((rows, rows), lambda h: (0, 0)), block],
        out_specs=block,
        out_shape=jax.ShapeDtypeStruct(queries.shape, bf16),
    )(onehot, home)


def solution(mesh):
    return jax.shard_map(
        per_device,
        mesh=mesh,
        in_specs=(
            P(("dp", "seq"), None),
            P(("dp", "seq"), None),
            P(("dp", "seq"), None),
            P(("dp", "seq")),
            P(("dp", "seq")),
        ),
        out_specs=P(("dp", "seq"), None),
        check_vma=False,
    )
```

profile of v0, /device:TPU:1, one launch (start us, length us, event | category | flops | bytes accessed | tf_op | source)
XLA Modules:
  0.0 120.7 jit_solution(2794263874513963063)
XLA Ops:
  0.0 1.2 %jit_solution_.3.freqs = f32[8,128]{1,0:T(8,128)} broadcast(f32[128]{0:T(128)} %constant.2.clone), dimensions={1} | broadcast | bytes 4608 | tf_op jit(solution)
  1.2 111.8 %shard_map.64 = (bf16[256,8192]{1,0:T(8,128)(2,1)}, bf16[256,256]{1,0:T(8,128)(2,1)}) custom-call(bf16[256,8192]{1,0:T(8,128)(2,1)} %q.1, bf16[256,1024]{1,0:T(8,128)(2,1)} %k.1, bf16[256,1024]{1,0:T(8,128)(2,1)} %v.1, s32[1,256]{1,0:T(1,128)} %bitcast.2, s32[1,256]{1,0:T(1,128)} %bitcast.3, f32[8,128]{1,0:T(8,128)} %jit_solution_.3.freqs), custom_call_target="tpu_custom_call" | custom-call | tf_op jit(solution)/shard_map/pallas_call | solution.py:352
  113.1 7.6 %shard_map.65 = bf16[256,8192]{1,0:T(8,128)(2,1)} custom-call(bf16[256,256]{1,0:T(8,128)(2,1)} %get-tuple-element.7.onehot, bf16[256,8192]{1,0:T(8,128)(2,1)} %get-tuple-element.8.home), custom_call_target="tpu_custom_call" | custom-call | tf_op jit(solution)/shard_map/pallas_call | solution.py:388
where the time goes:
time: 121 us
  Pallas kernels  119 us (98%)
  local copies, waits for them, and re-layouts  1.25 us (1%)
    pallas_call x1, Pallas kernels, per_device(): pl.pallas_call(functools.partial(travel, seqs, dps), in_specs=[anywhere,...  112 us
    pallas_call x1, Pallas kernels, per_device(): pl.pallas_call(restore, grid=(KVH,), in_specs=[pl.BlockSpec((rows, rows),...  7.58 us

commit v1 on v0

v1 whole, which is shorter than its diff:
```python
import functools

import jax
import jax.numpy as jnp
import numpy as np
from jax import lax
from jax.experimental import pallas as pl
from jax.experimental.pallas import tpu as pltpu
from jax.sharding import PartitionSpec as P

H = 64
KVH = 8
HD = 128
theta_base = 500000.0
UNIT = 128
LANES = 128
LOG2E = 1.4426950408889634
MESH = pl.DeviceIdType.MESH
CROSS = (((1,), (1,)), ((), ()))


def dot(a, b):
    return jnp.dot(a, b, preferred_element_type=jnp.float32)


def dot_t(a, b):
    return lax.dot_general(a, b, CROSS, preferred_element_type=jnp.float32)


def turn(x, c, s):
    return (x * c + pltpu.roll(x, HD // 2, 1) * s).astype(jnp.bfloat16)


def flip(d, w):
    return d + w * (1 - 2 * ((d // w) % 2))


def frequencies():
    exponents = np.arange(HD // 2, dtype=np.float32)
    return np.float32(theta_base) ** (np.float32(-2.0) * exponents / np.float32(HD))


def shared_bits(dps):
    return [w for w in (2, 4) if 2 * w <= dps]


def travel(
    seqs, dps, q, k, v, plan, seg, out,
    plan_v, seg_v, kraw, vraw, qs, kvs, qr, kvz, ob, home, ks, vs,
    onehot, onehot_t, sort, unsort, sort_half, unsort_half, bias, firsts, part_q,
    stiles, sgot, zspots, idz, idg,
    small_sem, kv_load, q_load,
    v_send, v_recv, v_own, k_send, k_recv, k_own,
    q_send, q_recv, q_own, o_send, o_recv, o_own,
    s_send, s_recv, iz_send, iz_recv, i_send, i_recv, zs_send, zs_recv, z_send, z_recv,
):
    rows = q.shape[0]
    per_kv = H // KVH
    wide = per_kv * HD
    chunk = rows // seqs
    share = chunk // dps
    slab = rows // dps
    group = rows * seqs
    upd = rows // UNIT
    hr = rows // 2
    bits = shared_bits(dps)
    nsh = len(bits)
    plain = KVH - nsh
    items = KVH + nsh
    half = dps // 2
    early = 4
    me = lax.axis_index("dp")
    z = lax.axis_index("seq")
    f32, bf16 = jnp.float32, jnp.bfloat16

    def remote(src, dst, send, recv, where):
        return pltpu.make_async_remote_copy(
            src_ref=src, dst_ref=dst, send_sem=send, recv_sem=recv,
            device_id=where, device_id_type=MESH,
        )

    def slab_of(d):
        return pl.ds(pl.multiple_of(d * slab, slab), slab)

    def cols(h, width):
        return pl.ds(pl.multiple_of(h * width, width), width)

    peers = [lax.rem(me + n, dps) for n in range(1, dps)]
    planes = [lax.rem(z + n, seqs) for n in range(1, seqs)]

    def rank_of(d, w):
        return (d // (2 * w)) * w + d % w

    def side(w):
        bit = (me // w) % 2
        inner = rank_of(me, w)
        found = []
        for n in range(1, half):
            c = lax.rem(inner + n, half)
            found.append((c // w) * (2 * w) + bit * w + c % w)
        return found

    smalls = [
        pltpu.make_async_copy(plan, plan_v, small_sem.at[0]),
        pltpu.make_async_copy(seg, seg_v, small_sem.at[1]),
    ]
    for copy in smalls:
        copy.start()
    v_load = pltpu.make_async_copy(v, vraw, kv_load.at[0])
    k_load = pltpu.make_async_copy(k, kraw, kv_load.at[1])
    v_load.start()
    k_load.start()

    barrier = pltpu.get_barrier_semaphore()

    for d in peers:
        pl.semaphore_signal(barrier, inc=1, device_id=(d, z), device_id_type=MESH)
    for p in planes:
        pl.semaphore_signal(barrier, inc=1, device_id=(me, p), device_id_type=MESH)

    def q_in(h):
        return pltpu.make_async_copy(q.at[:, cols(h, wide)], qs.at[h], q_load.at[h])

    @pl.loop(0, KVH)
    def _(h):
        q_in(h).start()

    lane = lax.broadcasted_iota(jnp.int32, (1, LANES), 1)
    smalls[1].wait()
    marks = jnp.zeros((1, LANES), f32)
    for u in range(upd):
        mine = seg_v[0:1, u * UNIT : u * UNIT + 1].astype(f32)
        marks = jnp.where(lane == z * upd + u, mine, marks)
    idz[z] = jnp.broadcast_to(marks, (8, LANES))

    row = lax.broadcasted_iota(jnp.int32, (rows, rows), 0)
    col = lax.broadcasted_iota(jnp.int32, (rows, rows), 1)
    eye = jnp.where(row == col, 1.0, 0.0).astype(bf16)
    smalls[0].wait()
    target = (plan_v[...] // rows).astype(f32)
    spread = jnp.broadcast_to(target, (16, rows)).astype(bf16)
    upright = dot_t(eye, spread)[:, 0:1]
    ahead = jnp.where((upright == target) & (row < col), 1.0, 0.0)
    slot = target * share + jnp.sum(ahead, axis=0, keepdims=True)
    place = jnp.where(slot == row.astype(f32), 1.0, 0.0).astype(bf16)
    onehot[...] = place
    onehot_t[...] = dot_t(eye, place).astype(bf16)

    spot = plan_v[...] % group
    high = jnp.broadcast_to((spot // 32).astype(f32), (8, rows))
    low = jnp.broadcast_to((spot % 32).astype(f32), (8, rows))
    lines = jnp.concatenate([high, low], axis=0).astype(bf16)
    flat = dot_t(lines, place)
    flat = flat[0:8] * 32.0 + flat[8:16]
    upright = dot_t(place, lines)
    spot_up = upright[:, 0:1] * 32.0 + upright[:, 8:9]
    sub = lax.broadcasted_iota(jnp.int32, (8, LANES), 0)
    shifted = [pltpu.roll(flat, (rows - d * slab) % rows, 1)[:, :LANES] for d in range(dps)]
    for d in range(dps):
        tile = shifted[d]
        for n, w in enumerate(bits):
            tile = jnp.where(sub == n + 1, shifted[flip(d, w)], tile)
        stiles[d] = tile
    sgot[me] = stiles[me]

    pl.semaphore_wait(barrier, dps + seqs - 2)

    def id_hop(n, p, origin):
        block = idz.at[origin]
        return remote(block, block, iz_send.at[n - 1], iz_recv.at[origin], (me, p))

    for n, p in enumerate(planes, 1):
        id_hop(n, p, z).start()

    for d in peers:
        remote(stiles.at[d], sgot.at[me], s_send, s_recv, (d, z)).start()

    most = pl.ds(0, rows - slab)
    lower, upper = pl.ds(0, HD), pl.ds(HD, HD)

    def kv_push(h, item, w, part, send, recv, own):
        for d in peers:
            origin = d if w == 0 else flip(d, w)
            remote(
                kvs.at[h, slab_of(origin), part], kvz.at[z, item, slab_of(me), part],
                send.at[item], recv.at[item], (d, z),
            ).start()
        kv_local(h, item, w, part, own).start()

    def kv_local(h, item, w, part, own):
        origin = me if w == 0 else flip(me, w)
        return pltpu.make_async_copy(
            kvs.at[h, slab_of(origin), part], kvz.at[z, item, slab_of(me), part], own.at[item]
        )

    def kv_all(item, part, send, recv):
        block = kvz.at[z, item, most, part]
        return remote(block, block, send.at[item], recv.at[item], (me, z))

    def kv_own(item, part, own):
        block = kvz.at[z, item, slab_of(me), part]
        return pltpu.make_async_copy(block, block, own.at[item])

    v_load.wait()

    def v_pair(pair):
        both = dot(onehot[...], vraw[:, cols(pair, 2 * HD)]).astype(bf16)
        for n in range(2):
            h = pair * 2 + n
            kvs[h, :, HD:] = both[:, n * HD : (n + 1) * HD]
            kv_push(h, h, 0, upper, v_send, v_recv, v_own)

    pl.loop(0, early // 2)(v_pair)

    for n, p in enumerate(planes, 1):
        id_hop(n, p, p).wait_recv()
    idg[me] = functools.reduce(jnp.add, [idz[p] for p in range(seqs)])
    for d in peers:
        remote(idg.at[me], idg.at[me], i_send, i_recv, (d, z)).start()

    pl.loop(early // 2, KVH // 2)(v_pair)

    for n, w in enumerate(bits):
        kv_push(plain + n, KVH + n, w, upper, v_send, v_recv, v_own)

    def hop(up, t, origin, item, part=None):
        step = 1 if up else -1
        block = kvz.at[origin, item] if part is None else kvz.at[origin, item, :, part]
        return remote(
            block, block,
            z_send.at[(0 if up else 1) * seqs + t, item], z_recv.at[origin, item], (me, z + step),
        )

    def leave(item, part):
        @pl.when(z + 1 < seqs)
        def _():
            hop(True, 0, z, item, part).start()

        @pl.when(z > 0)
        def _():
            hop(False, 0, z, item, part).start()

    def v_leave(item):
        kv_all(item, upper, v_send, v_recv).wait_recv()
        kv_own(item, upper, v_own).wait()
        leave(item, upper)

    pl.loop(0, early)(v_leave)

    def ids_all():
        some = idg.at[pl.ds(0, dps - 1)]
        return remote(some, some, i_send, i_recv, (me, z))

    ids_all().wait_recv()
    ids = jnp.concatenate([idg[d, 0:1, :] for d in range(dps)], axis=0)
    first = jnp.full((dps, LANES), float(group), f32)
    for u in range(seqs * upd):
        same = ids == ids[:, u : u + 1]
        first = jnp.where(same, jnp.minimum(first, float(u * UNIT)), first)
    firsts[...] = first

    def starts(spots, table):
        unit = jnp.floor(spots * (1.0 / UNIT))
        hit = lane.astype(f32) == unit
        return jnp.sum(jnp.where(hit, table, 0.0), axis=1, keepdims=True)

    freqs = jnp.zeros((1, HD), f32)
    for j, freq in enumerate(frequencies()):
        freqs = jnp.where(lane % (HD // 2) == j, freq, freqs)
    table = jnp.concatenate(
        [jnp.broadcast_to(first[d : d + 1], (slab, LANES)) for d in range(dps)], axis=0
    )
    angles = (spot_up - starts(spot_up, table)) * freqs
    cosine = jnp.cos(angles)
    sine = jnp.sin(angles) * jnp.where(lane < HD // 2, -1.0, 1.0)

    k_load.wait()

    @pl.loop(0, KVH // 2)
    def _(pair):
        both = dot(onehot[...], kraw[:, cols(pair, 2 * HD)])
        for n in range(2):
            h = pair * 2 + n
            kvs[h, :, :HD] = turn(both[:, n * HD : (n + 1) * HD], cosine, sine)
            kv_push(h, h, 0, lower, k_send, k_recv, k_own)

    for n, w in enumerate(bits):
        kv_push(plain + n, KVH + n, w, lower, k_send, k_recv, k_own)

    def spots_all():
        some = sgot.at[pl.ds(0, dps - 1)]
        return remote(some, some, s_send, s_recv, (me, z))

    spots_all().wait_recv()
    strips = []
    for start in range(0, rows, LANES):
        strip = jnp.zeros((8, LANES), f32)
        for d in range(start // slab, (start + LANES) // slab):
            off = d * slab - start
            inside = (lane >= off) & (lane < off + slab)
            strip = jnp.where(inside, pltpu.roll(sgot[d], off, 1) if off else sgot[d], strip)
        strips.append(strip)
    zspots[z] = jnp.concatenate(strips, axis=1)

    def spots_hop(n, p, origin):
        block = zspots.at[origin]
        return remote(block, block, zs_send.at[n - 1], zs_recv.at[origin], (me, p))

    for n, p in enumerate(planes, 1):
        spots_hop(n, p, z).start()

    pl.loop(early, items)(v_leave)

    def q_turn(h):
        q_in(h).wait()
        x = dot(onehot[...], qs[h])
        for g in range(per_kv):
            qs[h, :, g * HD : (g + 1) * HD] = turn(x[:, g * HD : (g + 1) * HD], cosine, sine)

    def q_plain(h):
        q_turn(h)
        for d in peers:
            remote(
                qs.at[h, slab_of(d)], qr.at[h, slab_of(me)],
                q_send.at[h], q_recv.at[h], (d, z),
            ).start()
        pltpu.make_async_copy(
            qs.at[h, slab_of(me)], qr.at[h, slab_of(me)], q_own.at[h]
        ).start()

    def spot_in(sel, rank):
        return pl.ds(pl.multiple_of(sel * hr + rank * slab, slab), slab)

    def q_shared(h, w):
        q_turn(h)
        for sel in range(2):
            for d in side(w):
                remote(
                    qs.at[h, slab_of(flip(d, w) if sel else d)], qr.at[h, spot_in(sel, rank_of(me, w))],
                    q_send.at[h], q_recv.at[h], (d, z),
                ).start()
            pltpu.make_async_copy(
                qs.at[h, slab_of(flip(me, w) if sel else me)], qr.at[h, spot_in(sel, rank_of(me, w))],
                q_own.at[h],
            ).start()

    def o_plain(h):
        for d in peers:
            remote(
                ob.at[h, slab_of(d)], home.at[h, slab_of(me)],
                o_send.at[h], o_recv.at[h], (d, z),
            ).start()
        pltpu.make_async_copy(
            ob.at[h, slab_of(me)], home.at[h, slab_of(me)], o_own.at[h]
        ).start()

    def o_shared(h, item, w, sel):
        target = slab_of(flip(me, w) if sel else me)
        for d in side(w):
            remote(
                ob.at[h, spot_in(sel, rank_of(d, w))], home.at[h, target],
                o_send.at[item], o_recv.at[item], (d, z),
            ).start()
        pltpu.make_async_copy(
            ob.at[h, spot_in(sel, rank_of(me, w))], home.at[h, target], o_own.at[item]
        ).start()

    def away(buf, h, index, send, recv, count):
        block = buf.at[h, pl.ds(0, count)]
        return remote(block, block, send.at[index], recv.at[index], (me, z))

    def stay(buf, h, index, own, count):
        block = buf.at[h, pl.ds(0, count)]
        return pltpu.make_async_copy(block, block, own.at[index])

    def arrival(s):
        inner = s % chunk
        return (inner // share) * (seqs * share) + (s // chunk) * share + inner % share

    def arrival_half(s):
        inner = s % (chunk // 2)
        return (inner // share) * slab + (s // (chunk // 2)) * share + inner % share

    def source_half(s, w):
        inner = s % (chunk // 2)
        rank = inner // share
        d = (rank // w) * (2 * w) + ((me // w) % 2) * w + rank % w
        return d * slab + (s // (chunk // 2)) * share + inner % share

    def orders():
        sort[...] = jnp.where(col == arrival(row), 1.0, 0.0).astype(bf16)
        unsort[...] = jnp.where(row == arrival(col), 1.0, 0.0).astype(bf16)
        row_half, col_half = row[:hr, :hr], col[:hr, :hr]
        sort_half[...] = jnp.where(col_half == arrival_half(row_half), 1.0, 0.0).astype(bf16)
        unsort_half[...] = jnp.where(row_half == arrival_half(col_half), 1.0, 0.0).astype(bf16)

    def halves(x):
        top = jnp.floor(x * (1.0 / 32.0))
        return jnp.concatenate([top, x - 32.0 * top], axis=0).astype(bf16)

    def prepare():
        for n, p in enumerate(planes, 1):
            spots_hop(n, p, p).wait_recv()
        planed = []
        for p in range(seqs):
            s = dot_t(halves(zspots[p]), sort[...])
            planed.append(s[0:8] * 32.0 + s[8:16])
        keyed = []
        for start in range(0, group, LANES):
            strip = jnp.zeros((8, LANES), f32)
            for piece in range(start // chunk, (start + LANES) // chunk):
                c, p = piece // seqs, piece % seqs
                source = c * chunk
                base = source // LANES * LANES
                off = piece * chunk - start
                moved = planed[p][:, base : base + LANES]
                shift = (off - (source - base)) % LANES
                if shift:
                    moved = pltpu.roll(moved, shift, 1)
                strip = jnp.where((lane >= off) & (lane < off + chunk), moved, strip)
            keyed.append(strip)
        key = jnp.concatenate(keyed, axis=1)

        def fence(order, low_row, count, spots, key_row, owner):
            begin = starts(spots, firsts[pl.ds(owner, 1), :])
            keep = (key[key_row : key_row + 1] <= spots) & (key[key_row : key_row + 1] >= begin)
            bias[order, low_row : low_row + count] = jnp.where(keep, 0.0, -1e30)

        here = halves(zspots[z])
        up = dot_t(sort[...], here)
        fence(0, 0, rows, up[:, 0:1] * 32.0 + up[:, 8:9], 0, me)
        for n, w in enumerate(bits):
            pick = jnp.where(col[:hr] == source_half(row[:hr], w), 1.0, 0.0).astype(bf16)
            up = dot_t(pick, here)
            fence(n + 1, 0, hr, up[:, 0:1] * 32.0 + up[:, 8:9], 0, me)
            m = n + 1
            spots = up[:, m : m + 1] * 32.0 + up[:, m + 8 : m + 9]
            fence(n + 1, hr, hr, spots, m, flip(me, w))

    def attend(h, item, order, base, count, forth, back):
        here = pl.ds(base, count)
        x = dot(forth[...], qr[h, here]).astype(bf16)
        piece = count // seqs
        for p in range(seqs):
            both = dot(sort[...], kvz[p, item]).astype(bf16)
            for c in range(seqs):
                spot_rows = slice(c * rows + p * chunk, c * rows + (p + 1) * chunk)
                ks[spot_rows] = both[c * chunk : (c + 1) * chunk, :HD]
                vs[spot_rows] = both[c * chunk : (c + 1) * chunk, HD:]
        for c in range(seqs):
            reach = (c + 1) * rows
            inner = slice(c * piece, (c + 1) * piece)
            block = jnp.concatenate(
                [x[inner, g * HD : (g + 1) * HD] for g in range(per_kv)], axis=0
            )
            s = dot_t(block, ks[:reach])
            s = s.reshape(per_kv, piece, reach) * (HD ** -0.5 * LOG2E)
            s = s + bias[order, pl.ds(base + c * piece, piece), :reach][None]
            e = jnp.exp2(s - jnp.max(s, axis=-1, keepdims=True))
            total = jnp.sum(e, axis=-1, keepdims=True).reshape(per_kv * piece, 1)
            mixed = dot(e.astype(bf16).reshape(per_kv * piece, reach), vs[:reach])
            mixed = (mixed / total).astype(bf16)
            for g in range(per_kv):
                part_q[inner, g * HD : (g + 1) * HD] = mixed[g * piece : (g + 1) * piece]
        ob[h, here] = dot(back[...], part_q[:count]).astype(bf16)

    def finish(h):
        away(home, h, h, o_send, o_recv, rows - slab).wait_recv()
        stay(home, h, h, o_own, slab).wait()
        out[:, cols(h, wide)] = dot(onehot_t[...], home[h]).astype(bf16)

    def finish_shared(h, n):
        for item in (h, KVH + n):
            away(home, h, item, o_send, o_recv, hr - slab).wait_recv()
            stay(home, h, item, o_own, slab).wait()
        out[:, cols(h, wide)] = dot(onehot_t[...], home[h]).astype(bf16)

    done = plain // 2

    @pl.loop(0, items + seqs - 1)
    def _(i):
        @pl.when(i < items)
        def _():
            kv_all(i, lower, k_send, k_recv).wait_recv()
            kv_own(i, lower, k_own).wait()
            leave(i, lower)

        for t in range(1, seqs):
            live = (i >= t) & (i - t < items)

            @pl.when(live & (z >= t))
            def _():
                hop(True, t, z - t, i - t).wait_recv()

                @pl.when(z + 1 < seqs)
                def _():
                    hop(True, t, z - t, i - t).start()

            @pl.when(live & (z + t < seqs))
            def _():
                hop(False, t, z + t, i - t).wait_recv()

                @pl.when(z > 0)
                def _():
                    hop(False, t, z + t, i - t).start()

        @pl.when(i < plain // 2)
        def _():
            q_plain(2 * i)
            q_plain(2 * i + 1)

        @pl.when(i == plain // 2)
        def _():
            for h in range(plain // 2 * 2, plain):
                q_plain(h)
            for n, w in enumerate(bits):
                q_shared(plain + n, w)

        @pl.when(i == min(2, seqs - 1))
        def _():
            orders()
            prepare()

        j = i - (seqs - 1)

        @pl.when((j >= 0) & (j < plain))
        def _():
            away(qr, j, j, q_send, q_recv, rows - slab).wait_recv()
            stay(qr, j, j, q_own, slab).wait()
            attend(j, j, 0, 0, rows, sort, unsort)
            o_plain(j)

        if nsh:
            @pl.when((j >= plain) & (j < KVH))
            def _():
                away(qr, j, j, q_send, q_recv, rows - 2 * slab).wait_recv()
                stay(qr, j, j, q_own, 2 * slab).wait()

            @pl.when(j >= plain)
            def _():
                n = (j - plain) % nsh
                sel = (j - plain) // nsh
                base = pl.multiple_of(sel * hr, hr)
                attend(plain + n, j, n + 1, base, hr, sort_half, unsort_half)

            for sel in range(2):
                for n, w in enumerate(bits):
                    @pl.when(j == plain + sel * nsh + n)
                    def _():
                        o_shared(plain + n, plain + sel * nsh + n, w, sel)

        @pl.when(i == items + seqs - 3)
        def _():
            pl.loop(0, done)(finish)

    pl.loop(done, plain)(finish)
    for n in range(nsh):
        finish_shared(plain + n, n)

    ids_all().wait_send()
    spots_all().wait_send()
    for n, p in enumerate(planes, 1):
        id_hop(n, p, z).wait_send()
        spots_hop(n, p, z).wait_send()

    @pl.loop(0, items)
    def _(item):
        kv_all(item, upper, v_send, v_recv).wait_send()
        kv_all(item, lower, k_send, k_recv).wait_send()
        for t in range(seqs - 1):

            @pl.when((z >= t) & (z + 1 < seqs))
            def _():
                hop(True, t, z - t, item).wait_send()

            @pl.when((z + t < seqs) & (z > 0))
            def _():
                hop(False, t, z + t, item).wait_send()

    @pl.loop(0, plain)
    def _(h):
        away(qr, h, h, q_send, q_recv, rows - slab).wait_send()
        away(ob, h, h, o_send, o_recv, rows - slab).wait_send()

    for n in range(nsh):
        h = plain + n
        away(qr, h, h, q_send, q_recv, rows - 2 * slab).wait_send()
        for item in (h, KVH + n):
            away(ob, h, item, o_send, o_recv, hr - slab).wait_send()


def per_device(queries, keys, values, plan, segment_ids):
    rows = queries.shape[0]
    seqs = lax.axis_size("seq")
    dps = lax.axis_size("dp")
    group = rows * seqs
    per_kv = H // KVH
    wide = per_kv * HD
    nsh = len(shared_bits(dps))
    items = KVH + nsh
    anywhere = pl.BlockSpec(memory_space=pltpu.HBM)
    dma = pltpu.SemaphoreType.DMA
    bf16, f32, i32 = jnp.bfloat16, jnp.float32, jnp.int32
    return pl.pallas_call(
        functools.partial(travel, seqs, dps),
        in_specs=[anywhere] * 5,
        out_specs=pl.BlockSpec(memory_space=pltpu.VMEM),
        out_shape=pltpu.VMEM(queries.shape, bf16),
        scratch_shapes=[
            pltpu.VMEM((1, rows), i32),
            pltpu.VMEM((1, rows), i32),
            pltpu.VMEM((rows, KVH * HD), bf16),
            pltpu.VMEM((rows, KVH * HD), bf16),
            pltpu.VMEM((KVH, rows, wide), bf16),
            pltpu.VMEM((KVH, rows, 2 * HD), bf16),
            pltpu.VMEM((KVH, rows, wide), bf16),
            pltpu.VMEM((seqs, items, rows, 2 * HD), bf16),
            pltpu.VMEM((KVH, rows, wide), bf16),
            pltpu.VMEM((KVH, rows, wide), bf16),
            pltpu.VMEM((group, HD), bf16),
            pltpu.VMEM((group, HD), bf16),
            pltpu.VMEM((rows, rows), bf16),
            pltpu.VMEM((rows, rows), bf16),
            pltpu.VMEM((rows, rows), bf16),
            pltpu.VMEM((rows, rows), bf16),
            pltpu.VMEM((rows // 2, rows // 2), bf16),
            pltpu.VMEM((rows // 2, rows // 2), bf16),
            pltpu.VMEM((1 + nsh, rows, group), f32),
            pltpu.VMEM((dps, LANES), f32),
            pltpu.VMEM((rows, wide), bf16),
            pltpu.VMEM((dps, 8, LANES), f32),
            pltpu.VMEM((dps, 8, LANES), f32),
            pltpu.VMEM((seqs, 8, rows), f32),
            pltpu.VMEM((seqs, 8, LANES), f32),
            pltpu.VMEM((dps, 8, LANES), f32),
            dma((2,)), dma((2,)), dma((KVH,)),
            dma((items,)), dma((items,)), dma((items,)),
            dma((items,)), dma((items,)), dma((items,)),
            dma((KVH,)), dma((KVH,)), dma((KVH,)),
            dma((items,)), dma((items,)), dma((items,)),
            dma, dma, dma((seqs,)), dma((seqs,)), dma, dma, dma((seqs,)), dma((seqs,)),
            dma((2 * seqs, items)), dma((seqs, items)),
        ],
        compiler_params=pltpu.CompilerParams(
            collective_id=0, has_side_effects=True, vmem_limit_bytes=56 * 1024 * 1024
        ),
    )(queries, keys, values, plan[None, :], segment_ids[None, :])


def solution(mesh):
    return jax.shard_map(
        per_device,
        mesh=mesh,
        in_specs=(
            P(("dp", "seq"), None),
            P(("dp", "seq"), None),
            P(("dp", "seq"), None),
            P(("dp", "seq")),
            P(("dp", "seq")),
        ),
        out_specs=P(("dp", "seq"), None),
        check_vma=False,
    )
```

time: 121 us -> 109 us (0.901)
  Pallas kernels: 119 us -> 107 us
    pallas_call x2 -> x1, Pallas kernels: 119 us -> 107 us  [per_device(): pl.pallas_call(functools.partial(travel, seqs, dps), in_specs=[anywhere]...]
    unnamed x0 -> x1, local copies, waits for them, and re-layouts: none -> 2.02 us
    another operation x1 -> x0, local copies, waits for them, and re-layouts: 1.25 us -> none
where the time goes in v1:
time: 109 us
  Pallas kernels  107 us (98%)
  local copies, waits for them, and re-layouts  2.02 us (2%)
    pallas_call x1, Pallas kernels, per_device(): pl.pallas_call(functools.partial(travel, seqs, dps), in_specs=[anywhere]...  107 us

profile of v1, /device:TPU:1, one launch (start us, length us, event | category | flops | bytes accessed | tf_op | source)
XLA Modules:
  0.0 109.0 jit_solution(11860463463535868873)
XLA Ops:
  0.0 107.0 %shard_map.55 = bf16[256,8192]{1,0:T(8,128)(2,1)S(1)} custom-call(bf16[256,8192]{1,0:T(8,128)(2,1)} %q.1, bf16[256,1024]{1,0:T(8,128)(2,1)} %k.1, bf16[256,1024]{1,0:T(8,128)(2,1)} %v.1, s32[1,256]{1,0:T(1,128)} %bitcast.2, s32[1,256]{1,0:T(1,128)} %bitcast.3), custom_call_target="tpu_custom_call" | custom-call | tf_op jit(solution)/shard_map/pallas_call | solution.py:604
  107.0 2.0 %copy.7 = bf16[256,8192]{1,0:T(8,128)(2,1)} copy(bf16[256,8192]{1,0:T(8,128)(2,1)S(1)} %shard_map.55) | data formatting | bytes 8388608

commit v2 on v1

--- a/solution.py
+++ b/solution.py
@@ -475,8 +475,6 @@
             stay(home, h, item, o_own, slab).wait()
         out[:, cols(h, wide)] = dot(onehot_t[...], home[h]).astype(bf16)
 
-    done = plain // 2
-
     @pl.loop(0, items + seqs - 1)
     def _(i):
         @pl.when(i < items)
@@ -549,11 +547,8 @@
                     def _():
                         o_shared(plain + n, plain + sel * nsh + n, w, sel)
 
-        @pl.when(i == items + seqs - 3)
-        def _():
-            pl.loop(0, done)(finish)
-
-    pl.loop(done, plain)(finish)
+
+    pl.loop(0, plain)(finish)
     for n in range(nsh):
         finish_shared(plain + n, n)
 

time: 109 us -> 108 us (level)
  no operation moved by 1% of the time
where the time goes in v2:
time: 108 us
  Pallas kernels  106 us (98%)
  local copies, waits for them, and re-layouts  2.02 us (2%)
    pallas_call x1, Pallas kernels, per_device(): pl.pallas_call(functools.partial(travel, seqs, dps), in_specs=[anywhere]...  106 us

profile of v2, /device:TPU:1, one launch (start us, length us, event | category | flops | bytes accessed | tf_op | source)
XLA Modules:
  0.0 108.1 jit_solution(7906883589676680420)
XLA Ops:
  0.0 106.1 %shard_map.55 = bf16[256,8192]{1,0:T(8,128)(2,1)S(1)} custom-call(bf16[256,8192]{1,0:T(8,128)(2,1)} %q.1, bf16[256,1024]{1,0:T(8,128)(2,1)} %k.1, bf16[256,1024]{1,0:T(8,128)(2,1)} %v.1, s32[1,256]{1,0:T(1,128)} %bitcast.2, s32[1,256]{1,0:T(1,128)} %bitcast.3), custom_call_target="tpu_custom_call" | custom-call | tf_op jit(solution)/shard_map/pallas_call | solution.py:599
  106.1 2.0 %copy.7 = bf16[256,8192]{1,0:T(8,128)(2,1)} copy(bf16[256,8192]{1,0:T(8,128)(2,1)S(1)} %shard_map.55) | data formatting | bytes 8388608
